TPU v7x, 128 devices: a whole 4x4x4 slice. The times are simulated.
128 devices in a mesh: ctx: 64 (over z, y, x), head: 2 (over core).
Axes of the slice: x: 4, y: 4, z: 4, core: 2. Of those that a mesh axis runs over, the one named last changes fastest.
Arguments:
- ssm_input: bfloat16 [16384, 4096], P('ctx', 'head'), may hold values from -6 to 6
- gate_input: bfloat16 [16384, 4096], P('ctx', 'head'), may hold values from -6 to 6
- b_input: bfloat16 [16384, 512], P('ctx', 'head'), may hold values from -0.375 to 0.375
- c_input: bfloat16 [16384, 512], P('ctx', 'head'), may hold values from -0.375 to 0.375
- step_size: float32 [16384, 64], P('ctx', 'head'), may hold values from 0.25 to 1
- decay_log: float32 [16384, 64], P('ctx', 'head'), may hold values from -0.8 to 0
- skip_gain: float32 [64], P('head'), may hold values from 0.1 to 1.9
- norm_gain: float32 [4096], P('head'), may hold values from 0.5 to 1.5
- queries: bfloat16 [16384, 8192], P('ctx', 'head'), may hold values from -240 to 240
- key_rows: bfloat16 [16384, 1024], P('ctx', 'head'), may hold values from -6 to 6
- value_rows: bfloat16 [16384, 1024], P('ctx', 'head'), may hold values from -6 to 6
- doc_lengths: int32 [32], replicated, may hold values from 1 to 1024, 16384 in all
Outputs:
- ssm_out: bfloat16 [16384, 4096], P('ctx', 'head')
- attn_out: bfloat16 [16384, 8192], P('ctx', 'head')
Inputs may be any that keep to these rules, and one draw needn't show every extreme that they name: `doc_lengths`: the 32 documents lie end to end and fill all 16384 tokens; the longest has exactly 1024 tokens.
All inputs are finite; a program needn't handle non-finite values.
Results may differ from a plain program's by a relative error of at most 0.005.
Values may be sent and summed in bfloat16 or wider, within the bound.
A program may use at most 256 MiB of HBM per device.

v0:
```python
import math

import jax
import jax.numpy as jnp
from jax import lax
from jax.experimental import pallas as pl
from jax.experimental.pallas import tpu as pltpu
from jax.sharding import PartitionSpec as P

ROWS = 256
BLK = 128
HP = 64
PAIRS = 16
LANES = 2048
EPS = 1e-05
CHANNELS = 4096
FAR = 2**30
SCALE = 1.0 / math.sqrt(128.0)
F32 = jnp.float32
BF16 = jnp.bfloat16
HIGH = lax.Precision.HIGHEST
MESH = pl.DeviceIdType.MESH
NT = (((1,), (1,)), ((), ()))
KV, ST, CR = 0, 1, 2
ORDER = ((KV, 0), (KV, 1), (CR, 0), (ST, 0), (ST, 1), (KV, 2), (KV, 3), (ST, 2), (ST, 3))
LEFT = ((KV, 0), (KV, 1), (ST, 0), (ST, 1))


def dot(a, b, precision=None):
    return jnp.dot(a, b, preferred_element_type=F32, precision=precision)


def dot_nt(a, b):
    return lax.dot_general(a, b, NT, preferred_element_type=F32)


def split3(v):
    hi = v.astype(BF16)
    rest = v - hi.astype(F32)
    mid = rest.astype(BF16)
    return hi, mid, (rest - mid.astype(F32)).astype(BF16)


def body(
    doc_ref, x_ref, b_ref, c_ref, step_ref, decay_ref, skip_ref, gain_ref, k_ref, v_ref, z_hbm, q_hbm,
    ssm_out, attn_out,
    z_ref, q_ref, kbuf, vbuf, tbuf, cbuf, town, cown, qaug, kaug, acc, peak,
    dpad, spad, cum_s, cum3, cum_t, step_t, end_t, scm, bt, intra, rgain, spread, bs0, enter0, enter1,
    sq_own, sq_other,
    lsem, kvs, kvr, sts, str_, qsem,
):
    d = lax.axis_index("ctx")
    head = lax.axis_index("head")
    n = lax.axis_size("ctx")
    x = lax.rem(d, 4)

    def at(off):
        return {"ctx": lax.rem(d + off + n, n)}

    right = {"ctx": jnp.where(x == 3, d - 3, d + 1)}
    left = {"ctx": jnp.where(x == 0, d + 3, d - 1)}
    other = {"head": 1 - head}
    z_copy = pltpu.make_async_copy(z_hbm, z_ref, lsem.at[0])
    q_copy = pltpu.make_async_copy(q_hbm, q_ref, lsem.at[1])
    q_copy.start()
    z_copy.start()
    barrier = pltpu.get_barrier_semaphore()
    for peer in (at(4), at(-4), at(1), at(-1), right, left, other):
        pl.semaphore_signal(barrier, inc=1, device_id=peer, device_id_type=MESH)
    pl.semaphore_wait(barrier, 7)

    def send(item, src, dist, to):
        kind, i = item
        s, r = dist - 1, dist - 1
        if kind == KV:
            lanes = pl.ds(i * 128, 128)
            pairs = ((k_ref, kbuf, 0), (v_ref, vbuf, 1))
            return [
                pltpu.make_async_remote_copy(
                    own.at[:, lanes] if src == 0 else buf.at[src - 1, :, lanes],
                    buf.at[dist - 1, :, lanes],
                    kvs.at[s, i, j], kvr.at[r, i, j], device_id=to, device_id_type=MESH,
                )
                for own, buf, j in pairs
            ]
        if kind == ST:
            lanes = pl.ds(i * 512, 512)
            return [
                pltpu.make_async_remote_copy(
                    town.at[:, lanes] if src == 0 else tbuf.at[src - 1, :, lanes],
                    tbuf.at[dist - 1, :, lanes],
                    sts.at[s, i], str_.at[r, i], device_id=to, device_id_type=MESH,
                )
            ]
        return [
            pltpu.make_async_remote_copy(
                cown if src == 0 else cbuf.at[src - 1], cbuf.at[dist - 1],
                sts.at[s, 4], str_.at[r, 4], device_id=to, device_id_type=MESH,
            )
        ]

    def start(copies):
        for copy in copies:
            copy.start()

    def arrive(item, dist):
        for copy in send(item, 0, dist, at(4)):
            copy.wait_recv()

    def send_own(items):
        for item in items:
            start(send(item, 0, 4, at(4)))

        @pl.when(x < 3)
        def _():
            for item in items:
                start(send(item, 0, 1, right))

        @pl.when(x == 0)
        def _():
            for item in items:
                start(send(item, 0, 3, left))

    def got4(item):
        arrive(item, 4)

        @pl.when(x > 0)
        def _():
            start(send(item, 4, 3, left))

        @pl.when(x == 3)
        def _():
            start(send(item, 4, 1, right))

    def got1(item):
        arrive(item, 1)
        if item not in LEFT:
            start(send(item, 1, 2, at(1)))

    def got3(item):
        arrive(item, 3)
        if item in LEFT:
            start(send(item, 3, 2, at(-1)))

    def got2(item):
        arrive(item, 2)

    send_own(ORDER[:2])

    lane = lax.broadcasted_iota(jnp.int32, (1, 128), 1)

    def one_doc(j, carry):
        run, first, last = carry
        length = doc_ref[j]
        first = jnp.where(lane == j, run, first)
        last = jnp.where(lane == j, run + length, last)
        return run + length, first, last

    first0 = jnp.where(lane == 127, -FAR, FAR)
    last0 = jnp.where(lane == 127, 0, -FAR)
    _, first, last = lax.fori_loop(0, 32, one_doc, (jnp.int32(0), first0, last0))

    def marks(base, rows):
        pos = base + lax.broadcasted_iota(jnp.int32, (rows, 128), 0)
        return jnp.where((pos >= first) & (pos < last), 1.0, 0.0).astype(F32)

    row0 = d * ROWS
    own_marks = marks(row0, ROWS)
    qaug[...] = ((own_marks - 1.0) * float(FAR)).astype(BF16)
    for j in range(5):
        kaug[j] = (own_marks if j == 0 else marks(row0 - j * ROWS, ROWS)).astype(BF16)

    dpad[...] = jnp.zeros_like(dpad)
    spad[...] = jnp.zeros_like(spad)
    dpad[:, 0:32] = decay_ref[...]
    spad[:, 0:32] = step_ref[...]
    ti = lax.broadcasted_iota(jnp.int32, (BLK, BLK), 0)
    si = lax.broadcasted_iota(jnp.int32, (BLK, BLK), 1)
    causal = ti >= si
    tri = causal.astype(F32)
    shift = [
        ((si == ti + 32 * k) & (ti < 32)).astype(BF16) for k in range(3)
    ]
    spread_i = lax.broadcasted_iota(jnp.int32, (BLK, LANES), 0)
    spread_l = lax.broadcasted_iota(jnp.int32, (BLK, LANES), 1)
    spread[...] = jnp.where(lax.shift_right_logical(spread_l, 6) == spread_i, 1.0, 0.0)
    carry_total = jnp.where(lane < 32, 1.0, 0.0)
    carry_rows = []
    for i in range(2):
        rows = slice(i * BLK, (i + 1) * BLK)
        oh = own_marks[rows]
        before = marks(row0 + i * BLK - 1, 8)[0:1]
        oh_last = oh[BLK - 1 : BLK]
        cum = dot(tri, dpad[rows], HIGH)
        cum_s[rows] = cum
        ct = cum.T
        cum_t[i] = ct
        stt = spad[rows].T
        step_t[i] = stt
        ohb = oh.astype(BF16)
        same = dot_nt(ohb, ohb)
        allowed = causal & (same > 0.5)
        last_row = same[BLK - 1 : BLK]
        end_t[i] = jnp.exp(ct[:, BLK - 1 : BLK] - ct) * last_row * stt
        for g in range(2):
            cols = slice(g * 128, (g + 1) * 128)
            sc = dot_nt(c_ref[rows, cols], b_ref[rows, cols])
            scm[2 * i + g] = jnp.where(allowed, sc, 0.0)
            bt[2 * i + g] = b_ref[rows, cols].astype(F32).T
        hi, mid, lo = split3(cum)
        cum3[rows] = (dot(hi, shift[0]) + dot(mid, shift[1]) + dot(lo, shift[2])).astype(BF16)
        joined = jnp.sum(oh_last * before, axis=1, keepdims=True)
        gain_row = jnp.where(lane < 32, jnp.exp(cum[BLK - 1 : BLK]) * joined, 0.0)
        carry_rows.append(gain_row)
        carry_total = carry_total * gain_row
        reads = jnp.sum(oh * before, axis=1, keepdims=True)
        rg = jnp.exp(cum) * reads
        rhi = rg.astype(BF16)
        rlo = (rg - rhi.astype(F32)).astype(BF16)
        e16 = spread[...].astype(BF16)
        rgain[rows] = dot(rhi, e16) + dot(rlo, e16)
    cown[...] = jnp.broadcast_to(carry_total, (8, 128))
    row_id = lax.broadcasted_iota(jnp.int32, (8, 128), 0)
    skip_pad = jnp.broadcast_to(skip_ref[...], (8, 128))
    small = jnp.where(row_id == 0, carry_rows[0], jnp.where(row_id == 1, carry_rows[1], skip_pad))
    wide = dot(small, spread[...], HIGH)
    carry0_w, carry1_w, skip_w = wide[0:1], wide[1:2], wide[2:3]
    spad[0:8] = small
    start_lane = lax.broadcasted_iota(jnp.int32, (BLK, 256), 1)
    start_row = lax.broadcasted_iota(jnp.int32, (BLK, 256), 0)
    low = lax.broadcasted_iota(jnp.int32, (BLK, BLK), 1) < HP
    enter0[0:8] = wide

    def pair(p, _):
        lanes = pl.ds(pl.multiple_of(p * 128, 128), 128)
        pick = jnp.where(
            ((start_row & 31) == 2 * p + lax.shift_right_logical(start_lane, 7)) & (start_row < 96), 1.0, 0.0
        ).astype(BF16)
        cols = dot(cum3[...], pick)
        g = lax.shift_right_logical(p, 3)
        outs = []
        for i in range(2):
            xs = x_ref[i * BLK : (i + 1) * BLK, lanes]
            parts = []
            sg = scm[2 * i + g]
            bg = bt[2 * i + g]
            for e in range(2):
                crow = cum_t[i, pl.ds(2 * p + e, 1), :]
                srow = step_t[i, pl.ds(2 * p + e, 1), :]
                diff = jnp.minimum(cols[i * BLK : (i + 1) * BLK, e * 128 : (e + 1) * 128] - crow, 0.0)
                parts.append((sg * jnp.exp(diff) * srow).astype(BF16))
            for e in range(2):
                erow = end_t[i, pl.ds(2 * p + e, 1), :]
                parts.append((bg * erow).astype(BF16))
            res = dot(jnp.concatenate(parts, axis=0), xs)
            intra[i * BLK : (i + 1) * BLK, lanes] = jnp.where(low, res[0:128], res[128:256])
            outs.append(jnp.where(low, res[256:384], res[384:512]))
        bs0[:, lanes] = outs[0]
        c1 = enter0[1:2, lanes]
        town[:, lanes] = (c1 * outs[0] + outs[1]).astype(BF16)
        return 0

    lax.fori_loop(0, PAIRS, pair, 0)
    send_own(ORDER[2:])
    q_copy.wait()

    def attend(g, dist):
        lanes = slice(g * 128, (g + 1) * 128)

        def one(r, _):
            h = g * 8 + r
            q = q_ref[:, pl.ds(pl.multiple_of(h * 128, 128), 128)]
            lhs = jnp.concatenate([q, qaug[...]], axis=1)
            if dist == 0:
                keys, values = k_ref[:, lanes], v_ref[:, lanes]
            else:
                keys, values = kbuf[dist - 1, :, lanes], vbuf[dist - 1, :, lanes]
            s = dot_nt(lhs, jnp.concatenate([keys, kaug[dist]], axis=1))
            if dist == 0:
                qi = lax.broadcasted_iota(jnp.int32, (ROWS, ROWS), 0)
                ki = lax.broadcasted_iota(jnp.int32, (ROWS, ROWS), 1)
                s = jnp.where(qi >= ki, s, -float(FAR))
            top = jnp.max(s, axis=1, keepdims=True)
            if dist == 0:
                new = jnp.broadcast_to(top, (ROWS, 128))
            else:
                old = peak[h]
                new = jnp.maximum(old, top)
            peak[h] = new
            prob = jnp.exp((s - jnp.concatenate([new, new], axis=1)) * SCALE).astype(BF16)
            out = dot(prob, jnp.concatenate([values, jnp.ones((ROWS, 128), BF16)], axis=1))
            if dist:
                back = jnp.exp((old - new) * SCALE)
                out = out + acc[h] * jnp.concatenate([back, back], axis=1)
            acc[h] = out
            return 0

        lax.fori_loop(0, 8, one, 0)

    def finish_ssm(quarter, squares):
        lo_l = quarter * 512
        lanes = slice(lo_l, lo_l + 512)
        state = tbuf[3, :, lanes].astype(F32)
        for dist in (3, 2, 1):
            cw = enter1[dist - 1 : dist, lanes]
            state = tbuf[dist - 1, :, lanes].astype(F32) + cw * state
        g = quarter // 2
        cols = slice(g * 128, (g + 1) * 128)
        later = enter0[0:1, lanes] * state + bs0[:, lanes]
        for i, st in enumerate((state, later)):
            rows = slice(i * BLK, (i + 1) * BLK)
            hi, mid, lo = split3(st)
            cc = c_ref[rows, cols]
            read = dot(jnp.concatenate([cc, cc], axis=1), jnp.concatenate([hi, mid], axis=0)) + dot(cc, lo)
            zz = z_ref[rows, lanes].astype(F32)
            y = intra[rows, lanes] + rgain[rows, lanes] * read
            y = y + enter0[2:3, lanes] * x_ref[rows, lanes].astype(F32)
            gated = y * (zz / (1.0 + jnp.exp(-zz)))
            intra[rows, lanes] = gated
            squares[i] = squares[i] + jnp.sum(gated * gated, axis=1, keepdims=True)
        return squares

    plan = {
        0: [(0, 0), (0, 4), (0, 1)],
        1: [(1, 0), (1, 4), (1, 1), (0, 3)],
        2: [(2, 0), (1, 3)],
        3: [],
        4: [(3, 0), (0, 2)],
        5: [(2, 4), (2, 1), (1, 2)],
        6: [(3, 4), (3, 1), (2, 3)],
        7: [(3, 3)],
        8: [],
    }
    early2 = {4: [(KV, 0)], 5: [(KV, 1)]}
    for i, item in enumerate(ORDER):
        got4(item)
        got1(item)
        if i:
            got3(ORDER[i - 1])
        for it in early2.get(i, ()):
            got2(it)
        for g, dist in plan[i]:
            attend(g, dist)
    got3(ORDER[-1])
    got2((CR, 0))
    rows8 = lax.broadcasted_iota(jnp.int32, (8, 128), 0)
    carries = jnp.where(rows8 == 0, cbuf[0], jnp.where(rows8 == 1, cbuf[1], cbuf[2]))
    enter1[...] = dot(carries, spread[...], HIGH)
    z_copy.wait()
    squares = [jnp.zeros((BLK, 1), F32)] * 2
    for quarter in (0, 1):
        got2((ST, quarter))
        squares = finish_ssm(quarter, squares)
    for g in (2, 3):
        got2((KV, g))
        attend(g, 2)
    for quarter in (2, 3):
        got2((ST, quarter))
        squares = finish_ssm(quarter, squares)
    for i in range(2):
        sq_own[i * BLK : (i + 1) * BLK] = jnp.broadcast_to(squares[i], (BLK, 128))

    sq_copy = pltpu.make_async_remote_copy(
        sq_own, sq_other, qsem.at[0], qsem.at[1], device_id=other, device_id_type=MESH
    )
    sq_copy.start()

    def divide(h, _):
        lanes = pl.ds(pl.multiple_of(h * 128, 128), 128)
        attn_out[:, lanes] = (acc[h, :, 0:128] / acc[h, :, 128:256]).astype(BF16)
        return 0

    lax.fori_loop(0, 32, divide, 0)
    sq_copy.wait()
    for i in range(2):
        rows = slice(i * BLK, (i + 1) * BLK)
        total = (sq_own[rows] + sq_other[rows])[:, 0:1]
        norm = lax.rsqrt(total / CHANNELS + EPS)
        ssm_out[rows] = (intra[rows] * norm * gain_ref[...]).astype(BF16)
    for dist in (1, 2, 3, 4):
        for item in ORDER:
            for copy in send(item, 0, dist, at(4)):
                copy.wait_send()


def per_device(
    ssm_input, gate_input, b_input, c_input, step_size, decay_log, skip_gain, norm_gain, queries, key_rows,
    value_rows, doc_lengths,
):
    vm = pl.BlockSpec(memory_space=pltpu.VMEM)
    hbm = pl.BlockSpec(memory_space=pl.ANY)
    sm = pl.BlockSpec(memory_space=pltpu.SMEM)
    dma = pltpu.SemaphoreType.DMA
    skip = jnp.pad(skip_gain, (0, 96)).reshape(1, 128)
    return pl.pallas_call(
        body,
        out_shape=(
            jax.ShapeDtypeStruct((ROWS, LANES), BF16),
            jax.ShapeDtypeStruct((ROWS, 4096), BF16),
        ),
        in_specs=[sm] + [vm] * 9 + [hbm] * 2,
        out_specs=(vm, vm),
        scratch_shapes=[
            pltpu.VMEM((ROWS, LANES), BF16),
            pltpu.VMEM((ROWS, 4096), BF16),
            pltpu.VMEM((4, ROWS, 512), BF16),
            pltpu.VMEM((4, ROWS, 512), BF16),
            pltpu.VMEM((4, BLK, LANES), BF16),
            pltpu.VMEM((4, 8, 128), F32),
            pltpu.VMEM((BLK, LANES), BF16),
            pltpu.VMEM((8, 128), F32),
            pltpu.VMEM((ROWS, 128), BF16),
            pltpu.VMEM((5, ROWS, 128), BF16),
            pltpu.VMEM((32, ROWS, 256), F32),
            pltpu.VMEM((32, ROWS, 128), F32),
            pltpu.VMEM((ROWS, 128), F32),
            pltpu.VMEM((ROWS, 128), F32),
            pltpu.VMEM((ROWS, 128), F32),
            pltpu.VMEM((ROWS, 128), BF16),
            pltpu.VMEM((2, 128, 128), F32),
            pltpu.VMEM((2, 128, 128), F32),
            pltpu.VMEM((2, 128, 128), F32),
            pltpu.VMEM((4, 128, 128), F32),
            pltpu.VMEM((4, 128, 128), F32),
            pltpu.VMEM((ROWS, LANES), F32),
            pltpu.VMEM((ROWS, LANES), F32),
            pltpu.VMEM((BLK, LANES), F32),
            pltpu.VMEM((BLK, LANES), F32),
            pltpu.VMEM((8, LANES), F32),
            pltpu.VMEM((8, LANES), F32),
            pltpu.VMEM((ROWS, 128), F32),
            pltpu.VMEM((ROWS, 128), F32),
            dma((2,)),
            dma((4, 4, 2)),
            dma((4, 4, 2)),
            dma((4, 5)),
            dma((4, 5)),
            dma((2,)),
        ],
        compiler_params=pltpu.CompilerParams(collective_id=0, has_side_effects=True),
        name="layer",
    )(
        doc_lengths, ssm_input, b_input, c_input, step_size, decay_log, skip, norm_gain.reshape(1, LANES),
        key_rows, value_rows, gate_input, queries,
    )


def solution(mesh):
    both = P("ctx", "head")
    placed = (both,) * 6 + (P("head"),) * 2 + (both,) * 3 + (P(),)
    return jax.shard_map(
        per_device, mesh=mesh, in_specs=placed, out_specs=(both, both), check_vma=False
    )
```

profile of v0, /device:TPU:1, one launch (start us, length us, event | category | flops | bytes accessed | tf_op | source)
XLA Modules:
  0.0 116.6 jit_solution(16197221861757978300)
XLA Ops:
  0.6 1.3 %pad_bitcast_fusion.skip_ref = f32[1,128]{1,0:T(1,128)} fusion(f32[32]{0:T(128)} %param.18), kind=kLoop, calls=%fused_computation | loop fusion | bytes 640 | tf_op jit(solution)/shard_map/reshape | solution.py:394
  1.9 1.5 %copy.14.step_ref = f32[256,32]{1,0:T(8,128)} copy(f32[256,32]{0,1:T(8,128)} %param.16) | data formatting | bytes 65536 | tf_op args[4]
  3.4 1.5 %copy.15.decay_ref = f32[256,32]{1,0:T(8,128)} copy(f32[256,32]{0,1:T(8,128)} %param.17) | data formatting | bytes 65536 | tf_op args[5]
  4.9 107.9 %layer.1 = (bf16[256,2048]{1,0:T(8,128)(2,1)}, bf16[256,4096]{1,0:T(8,128)(2,1)}) custom-call(s32[32]{0:T(128)} %doc_ref.1, bf16[256,2048]{1,0:T(8,128)(2,1)} %x_ref.1, bf16[256,256]{1,0:T(8,128)(2,1)} %b_ref.1, bf16[256,256]{1,0:T(8,128)(2,1)} %c_ref.1, f32[256,32]{1,0:T(8,128)} %copy.14.step_ref, f32[256,32]{1,0:T(8,128)} %copy.15.decay_ref, ...), custom_call_target="tpu_custom_call" | custom-call | tf_op jit(solution)/shard_map/layer/pallas_call | solution.py:395
  112.8 0.0 copy-start
  112.8 2.5 %copy.18 = bf16[256,2048]{1,0:T(8,128)(2,1)} copy(bf16[256,2048]{1,0:T(8,128)(2,1)} %get-tuple-element.4) | data formatting | bytes 2097152
  115.3 0.0 copy-done
  115.3 1.3 %copy.19 = bf16[256,4096]{1,0:T(8,128)(2,1)} copy(bf16[256,4096]{1,0:T(8,128)(2,1)S(1)} %copy-done) | data formatting | bytes 4194304
Async XLA Ops:
  112.8 2.5 %copy-start = (bf16[256,4096]{1,0:T(8,128)(2,1)S(1)}, bf16[256,4096]{1,0:T(8,128)(2,1)}, u32[]{:S(2)}) copy-start(bf16[256,4096]{1,0:T(8,128)(2,1)} %get-tuple-element.5) | copy-start | bytes 6291460
where the time goes:
time: 117 us
  Pallas kernels  108 us (92%)
  local copies, waits for them, and re-layouts  8.05 us (7%)
    pallas_call x1, Pallas kernels, per_device(): pl.pallas_call(body, out_shape=(jax.ShapeDtypeStruct((ROWS, LANES), BF16)...  108 us
    unnamed x6, local copies, waits for them, and re-layouts  6.8 us

commit v1 on v0

--- a/solution.py
+++ b/solution.py
@@ -15,14 +15,15 @@
 EPS = 1e-05
 CHANNELS = 4096
 FAR = 2**30
-SCALE = 1.0 / math.sqrt(128.0)
+SCALE2 = math.log2(math.e) / math.sqrt(128.0)
+UNROLL = 4
 F32 = jnp.float32
 BF16 = jnp.bfloat16
 HIGH = lax.Precision.HIGHEST
 MESH = pl.DeviceIdType.MESH
 NT = (((1,), (1,)), ((), ()))
 KV, ST, CR = 0, 1, 2
-ORDER = ((KV, 0), (KV, 1), (CR, 0), (ST, 0), (ST, 1), (KV, 2), (KV, 3), (ST, 2), (ST, 3))
+ORDER = ((KV, 0), (KV, 1), (KV, 2), (CR, 0), (ST, 0), (ST, 1), (KV, 3), (ST, 2), (ST, 3))
 LEFT = ((KV, 0), (KV, 1), (ST, 0), (ST, 1))
 
 
@@ -45,7 +46,7 @@
     doc_ref, x_ref, b_ref, c_ref, step_ref, decay_ref, skip_ref, gain_ref, k_ref, v_ref, z_hbm, q_hbm,
     ssm_out, attn_out,
     z_ref, q_ref, kbuf, vbuf, tbuf, cbuf, town, cown, qaug, kaug, acc, peak,
-    dpad, spad, cum_s, cum3, cum_t, step_t, end_t, scm, bt, intra, rgain, spread, bs0, enter0, enter1,
+    dpad, spad, skip_pad, cum3, cum_t, step_t, end_t, scm, bt, intra, rgain, spread, bs0, enter0, enter1,
     sq_own, sq_other,
     lsem, kvs, kvr, sts, str_, qsem,
 ):
@@ -145,7 +146,7 @@
     def got2(item):
         arrive(item, 2)
 
-    send_own(ORDER[:2])
+    send_own(ORDER[:3])
 
     lane = lax.broadcasted_iota(jnp.int32, (1, 128), 1)
 
@@ -172,8 +173,8 @@
 
     dpad[...] = jnp.zeros_like(dpad)
     spad[...] = jnp.zeros_like(spad)
-    dpad[:, 0:32] = decay_ref[...]
-    spad[:, 0:32] = step_ref[...]
+    dpad[0:32] = decay_ref[...]
+    spad[0:32] = step_ref[...]
     ti = lax.broadcasted_iota(jnp.int32, (BLK, BLK), 0)
     si = lax.broadcasted_iota(jnp.int32, (BLK, BLK), 1)
     causal = ti >= si
@@ -183,7 +184,13 @@
     ]
     spread_i = lax.broadcasted_iota(jnp.int32, (BLK, LANES), 0)
     spread_l = lax.broadcasted_iota(jnp.int32, (BLK, LANES), 1)
-    spread[...] = jnp.where(lax.shift_right_logical(spread_l, 6) == spread_i, 1.0, 0.0)
+    spread[...] = jnp.where(lax.shift_right_logical(spread_l, 6) == spread_i, 1.0, 0.0).astype(BF16)
+
+    def widen(rows8):
+        hi, mid, lo = split3(jnp.concatenate([rows8, jnp.zeros_like(rows8)], axis=0))
+        wide3 = dot(jnp.concatenate([hi, mid, lo], axis=0), spread[...])
+        return wide3[0:8] + wide3[16:24] + wide3[32:40]
+
     carry_total = jnp.where(lane < 32, 1.0, 0.0)
     carry_rows = []
     for i in range(2):
@@ -191,11 +198,10 @@
         oh = own_marks[rows]
         before = marks(row0 + i * BLK - 1, 8)[0:1]
         oh_last = oh[BLK - 1 : BLK]
-        cum = dot(tri, dpad[rows], HIGH)
-        cum_s[rows] = cum
-        ct = cum.T
+        ct = lax.dot_general(dpad[:, rows], tri, NT, preferred_element_type=F32, precision=HIGH)
+        cum = ct.T
         cum_t[i] = ct
-        stt = spad[rows].T
+        stt = spad[:, rows]
         step_t[i] = stt
         ohb = oh.astype(BF16)
         same = dot_nt(ohb, ohb)
@@ -217,15 +223,13 @@
         rg = jnp.exp(cum) * reads
         rhi = rg.astype(BF16)
         rlo = (rg - rhi.astype(F32)).astype(BF16)
-        e16 = spread[...].astype(BF16)
-        rgain[rows] = dot(rhi, e16) + dot(rlo, e16)
+        rgain[rows] = dot(rhi, spread[...]) + dot(rlo, spread[...])
     cown[...] = jnp.broadcast_to(carry_total, (8, 128))
     row_id = lax.broadcasted_iota(jnp.int32, (8, 128), 0)
-    skip_pad = jnp.broadcast_to(skip_ref[...], (8, 128))
-    small = jnp.where(row_id == 0, carry_rows[0], jnp.where(row_id == 1, carry_rows[1], skip_pad))
-    wide = dot(small, spread[...], HIGH)
-    carry0_w, carry1_w, skip_w = wide[0:1], wide[1:2], wide[2:3]
-    spad[0:8] = small
+    skip_pad[...] = jnp.zeros_like(skip_pad)
+    skip_pad[:, 0:32] = jnp.broadcast_to(skip_ref[...], (8, 32))
+    small = jnp.where(row_id == 0, carry_rows[0], jnp.where(row_id == 1, carry_rows[1], skip_pad[...]))
+    wide = widen(small)
     start_lane = lax.broadcasted_iota(jnp.int32, (BLK, 256), 1)
     start_row = lax.broadcasted_iota(jnp.int32, (BLK, 256), 0)
     low = lax.broadcasted_iota(jnp.int32, (BLK, BLK), 1) < HP
@@ -261,41 +265,61 @@
         return 0
 
     lax.fori_loop(0, PAIRS, pair, 0)
-    send_own(ORDER[2:])
+    send_own(ORDER[3:6])
     q_copy.wait()
 
-    def attend(g, dist):
+    def attend(g, parts, first_time):
         lanes = slice(g * 128, (g + 1) * 128)
-
-        def one(r, _):
-            h = g * 8 + r
-            q = q_ref[:, pl.ds(pl.multiple_of(h * 128, 128), 128)]
-            lhs = jnp.concatenate([q, qaug[...]], axis=1)
-            if dist == 0:
-                keys, values = k_ref[:, lanes], v_ref[:, lanes]
-            else:
-                keys, values = kbuf[dist - 1, :, lanes], vbuf[dist - 1, :, lanes]
-            s = dot_nt(lhs, jnp.concatenate([keys, kaug[dist]], axis=1))
-            if dist == 0:
-                qi = lax.broadcasted_iota(jnp.int32, (ROWS, ROWS), 0)
-                ki = lax.broadcasted_iota(jnp.int32, (ROWS, ROWS), 1)
-                s = jnp.where(qi >= ki, s, -float(FAR))
-            top = jnp.max(s, axis=1, keepdims=True)
-            if dist == 0:
-                new = jnp.broadcast_to(top, (ROWS, 128))
-            else:
-                old = peak[h]
-                new = jnp.maximum(old, top)
-            peak[h] = new
-            prob = jnp.exp((s - jnp.concatenate([new, new], axis=1)) * SCALE).astype(BF16)
-            out = dot(prob, jnp.concatenate([values, jnp.ones((ROWS, 128), BF16)], axis=1))
-            if dist:
-                back = jnp.exp((old - new) * SCALE)
-                out = out + acc[h] * jnp.concatenate([back, back], axis=1)
-            acc[h] = out
-            return 0
-
-        lax.fori_loop(0, 8, one, 0)
+        for half in range(2):
+            rows = slice(half * BLK, (half + 1) * BLK)
+
+            def one(r, _):
+                h = g * 8 + 2 * r
+                slot = half * 16 + g * 4 + r
+                qs, ks, vs, ms = [], [], [], []
+                for e in range(2):
+                    q = q_ref[rows, pl.ds(pl.multiple_of((h + e) * 128, 128), 128)]
+                    qs.append(jnp.concatenate([q, qaug[rows]], axis=1))
+                for dist, a, b in parts[half]:
+                    if dist == 0:
+                        keys, values = k_ref[a:b, lanes], v_ref[a:b, lanes]
+                    else:
+                        keys, values = kbuf[dist - 1, a:b, lanes], vbuf[dist - 1, a:b, lanes]
+                    ks.append(jnp.concatenate([keys, kaug[dist, a:b]], axis=1))
+                    vs.append(values)
+                values = jnp.concatenate(vs, axis=0)
+                s = dot_nt(jnp.concatenate(qs, axis=0), jnp.concatenate(ks, axis=0))
+                if first_time:
+                    at0 = half * BLK
+                    qi = lax.broadcasted_iota(jnp.int32, (2 * BLK, BLK), 0) & (BLK - 1)
+                    ki = lax.broadcasted_iota(jnp.int32, (2 * BLK, BLK), 1)
+                    diag = jnp.where(qi >= ki, s[:, at0 : at0 + BLK], -float(FAR))
+                    pieces = ([s[:, :at0]] if at0 else []) + [diag, s[:, at0 + BLK :]]
+                    s = jnp.concatenate(pieces, axis=1)
+                top = jnp.max(s, axis=1, keepdims=True)
+                if first_time:
+                    new = jnp.broadcast_to(top, (2 * BLK, 128))
+                else:
+                    old = peak[slot]
+                    new = jnp.maximum(old, top)
+                peak[slot] = new
+                wide_new = jnp.concatenate([new] * (s.shape[1] // 128), axis=1)
+                prob = jnp.exp2((s - wide_new) * SCALE2).astype(BF16)
+                ones = jnp.ones((values.shape[0], 128), BF16)
+                out = dot(prob, jnp.concatenate([values, ones], axis=1))
+                if not first_time:
+                    back = jnp.exp2((old - new) * SCALE2)
+                    out = out + acc[slot] * jnp.concatenate([back, back], axis=1)
+                acc[slot] = out
+                return 0
+
+            lax.fori_loop(0, 4, one, 0, unroll=UNROLL)
+
+    near = (
+        ((0, 0, 128), (4, 0, 256), (1, 0, 256)),
+        ((0, 0, 256), (4, 128, 256), (1, 0, 256)),
+    )
+    rest = (((3, 0, 256), (2, 0, 256)),) * 2
 
     def finish_ssm(quarter, squares):
         lo_l = quarter * 512
@@ -309,9 +333,10 @@
         later = enter0[0:1, lanes] * state + bs0[:, lanes]
         for i, st in enumerate((state, later)):
             rows = slice(i * BLK, (i + 1) * BLK)
-            hi, mid, lo = split3(st)
+            hi = st.astype(BF16)
+            mid = (st - hi.astype(F32)).astype(BF16)
             cc = c_ref[rows, cols]
-            read = dot(jnp.concatenate([cc, cc], axis=1), jnp.concatenate([hi, mid], axis=0)) + dot(cc, lo)
+            read = dot(jnp.concatenate([cc, cc], axis=1), jnp.concatenate([hi, mid], axis=0))
             zz = z_ref[rows, lanes].astype(F32)
             y = intra[rows, lanes] + rgain[rows, lanes] * read
             y = y + enter0[2:3, lanes] * x_ref[rows, lanes].astype(F32)
@@ -320,32 +345,25 @@
             squares[i] = squares[i] + jnp.sum(gated * gated, axis=1, keepdims=True)
         return squares
 
-    plan = {
-        0: [(0, 0), (0, 4), (0, 1)],
-        1: [(1, 0), (1, 4), (1, 1), (0, 3)],
-        2: [(2, 0), (1, 3)],
-        3: [],
-        4: [(3, 0), (0, 2)],
-        5: [(2, 4), (2, 1), (1, 2)],
-        6: [(3, 4), (3, 1), (2, 3)],
-        7: [(3, 3)],
-        8: [],
-    }
-    early2 = {4: [(KV, 0)], 5: [(KV, 1)]}
+    near_at = {0: 0, 1: 1, 2: 2, 6: 3}
+    rest_at = {7: 0, 8: 1}
     for i, item in enumerate(ORDER):
         got4(item)
         got1(item)
         if i:
             got3(ORDER[i - 1])
-        for it in early2.get(i, ()):
-            got2(it)
-        for g, dist in plan[i]:
-            attend(g, dist)
+        if i < 3:
+            send_own(ORDER[6 + i : 7 + i])
+        if i in near_at:
+            attend(near_at[i], near, True)
+        if i in rest_at:
+            got2((KV, rest_at[i]))
+            attend(rest_at[i], rest, False)
     got3(ORDER[-1])
     got2((CR, 0))
     rows8 = lax.broadcasted_iota(jnp.int32, (8, 128), 0)
     carries = jnp.where(rows8 == 0, cbuf[0], jnp.where(rows8 == 1, cbuf[1], cbuf[2]))
-    enter1[...] = dot(carries, spread[...], HIGH)
+    enter1[...] = widen(carries)
     z_copy.wait()
     squares = [jnp.zeros((BLK, 1), F32)] * 2
     for quarter in (0, 1):
@@ -353,7 +371,7 @@
         squares = finish_ssm(quarter, squares)
     for g in (2, 3):
         got2((KV, g))
-        attend(g, 2)
+        attend(g, rest, False)
     for quarter in (2, 3):
         got2((ST, quarter))
         squares = finish_ssm(quarter, squares)
@@ -365,12 +383,17 @@
     )
     sq_copy.start()
 
-    def divide(h, _):
-        lanes = pl.ds(pl.multiple_of(h * 128, 128), 128)
-        attn_out[:, lanes] = (acc[h, :, 0:128] / acc[h, :, 128:256]).astype(BF16)
+    def divide(t, _):
+        for half in range(2):
+            rows = slice(half * BLK, (half + 1) * BLK)
+            slot = half * 16 + t
+            for e in range(2):
+                part = slice(e * BLK, (e + 1) * BLK)
+                lanes = pl.ds(pl.multiple_of((2 * t + e) * 128, 128), 128)
+                attn_out[rows, lanes] = (acc[slot, part, 0:128] / acc[slot, part, 128:256]).astype(BF16)
         return 0
 
-    lax.fori_loop(0, 32, divide, 0)
+    lax.fori_loop(0, 16, divide, 0)
     sq_copy.wait()
     for i in range(2):
         rows = slice(i * BLK, (i + 1) * BLK)
@@ -391,7 +414,7 @@
     hbm = pl.BlockSpec(memory_space=pl.ANY)
     sm = pl.BlockSpec(memory_space=pltpu.SMEM)
     dma = pltpu.SemaphoreType.DMA
-    skip = jnp.pad(skip_gain, (0, 96)).reshape(1, 128)
+    skip = skip_gain.reshape(1, 32)
     return pl.pallas_call(
         body,
         out_shape=(
@@ -413,9 +436,9 @@
             pltpu.VMEM((5, ROWS, 128), BF16),
             pltpu.VMEM((32, ROWS, 256), F32),
             pltpu.VMEM((32, ROWS, 128), F32),
-            pltpu.VMEM((ROWS, 128), F32),
-            pltpu.VMEM((ROWS, 128), F32),
-            pltpu.VMEM((ROWS, 128), F32),
+            pltpu.VMEM((128, ROWS), F32),
+            pltpu.VMEM((128, ROWS), F32),
+            pltpu.VMEM((8, 128), F32),
             pltpu.VMEM((ROWS, 128), BF16),
             pltpu.VMEM((2, 128, 128), F32),
             pltpu.VMEM((2, 128, 128), F32),
@@ -424,7 +447,7 @@
             pltpu.VMEM((4, 128, 128), F32),
             pltpu.VMEM((ROWS, LANES), F32),
             pltpu.VMEM((ROWS, LANES), F32),
-            pltpu.VMEM((BLK, LANES), F32),
+            pltpu.VMEM((BLK, LANES), BF16),
             pltpu.VMEM((BLK, LANES), F32),
             pltpu.VMEM((8, LANES), F32),
             pltpu.VMEM((8, LANES), F32),
@@ -440,7 +463,7 @@
         compiler_params=pltpu.CompilerParams(collective_id=0, has_side_effects=True),
         name="layer",
     )(
-        doc_lengths, ssm_input, b_input, c_input, step_size, decay_log, skip, norm_gain.reshape(1, LANES),
+        doc_lengths, ssm_input, b_input, c_input, step_size.T, decay_log.T, skip, norm_gain.reshape(1, LANES),
         key_rows, value_rows, gate_input, queries,
     )
 

time: 117 us -> 68.2 us (0.58)
  Pallas kernels: 108 us -> 63.7 us
  local copies, waits for them, and re-layouts: 8.05 us -> 3.78 us
    pallas_call x1, Pallas kernels: 108 us -> 63.7 us  [per_device(): pl.pallas_call(body, out_shape=(jax.ShapeDtypeStruct((ROWS, LANES), BF16)...]
    unnamed x6 -> x4, local copies, waits for them, and re-layouts: 6.8 us -> 3.78 us
    reshape x1 -> x0, local copies, waits for them, and re-layouts: 1.25 us -> none  [per_device(): skip = jnp.pad(skip_gain, (0, 96)).reshape(1, 128)]
where the time goes in v1:
time: 68.2 us; the launch traced here: 68.1 us
  Pallas kernels  63.7 us (93%)
  local copies, waits for them, and re-layouts  3.78 us (6%)
    pallas_call x1, Pallas kernels, per_device(): pl.pallas_call(body, out_shape=(jax.ShapeDtypeStruct((ROWS, LANES), BF16)...  63.7 us
    unnamed x4, local copies, waits for them, and re-layouts  3.78 us

profile of v1, /device:TPU:1, one launch (start us, length us, event | category | flops | bytes accessed | tf_op | source)
XLA Modules:
  0.0 68.1 jit_solution(14403684525294040964)
XLA Ops:
  0.6 63.7 %layer.1 = (bf16[256,2048]{1,0:T(8,128)(2,1)}, bf16[256,4096]{1,0:T(8,128)(2,1)}) custom-call(s32[32]{0:T(128)} %doc_ref.1, bf16[256,2048]{1,0:T(8,128)(2,1)} %x_ref.1, bf16[256,256]{1,0:T(8,128)(2,1)} %b_ref.1, bf16[256,256]{1,0:T(8,128)(2,1)} %c_ref.1, f32[32,256]{1,0:T(8,128)} %bitcast.4, f32[32,256]{1,0:T(8,128)} %bitcast.5, f32[1,32]{1,0:T(1,128)} %bitcast.7, ...), custom_call_target="tpu_custom_call" | custom-call | tf_op jit(solution)/shard_map/layer/pallas_call | solution.py:418
  64.3 0.0 copy-start
  64.3 2.5 %copy.16 = bf16[256,2048]{1,0:T(8,128)(2,1)} copy(bf16[256,2048]{1,0:T(8,128)(2,1)} %get-tuple-element.4) | data formatting | bytes 2097152
  66.8 0.0 copy-done
  66.8 1.3 %copy.17 = bf16[256,4096]{1,0:T(8,128)(2,1)} copy(bf16[256,4096]{1,0:T(8,128)(2,1)S(1)} %copy-done) | data formatting | bytes 4194304
Async XLA Ops:
  64.3 2.5 %copy-start = (bf16[256,4096]{1,0:T(8,128)(2,1)S(1)}, bf16[256,4096]{1,0:T(8,128)(2,1)}, u32[]{:S(2)}) copy-start(bf16[256,4096]{1,0:T(8,128)(2,1)} %get-tuple-element.5) | copy-start | bytes 6291460

commit v2 on v1

--- a/solution.py
+++ b/solution.py
@@ -23,7 +23,7 @@
 MESH = pl.DeviceIdType.MESH
 NT = (((1,), (1,)), ((), ()))
 KV, ST, CR = 0, 1, 2
-ORDER = ((KV, 0), (KV, 1), (KV, 2), (CR, 0), (ST, 0), (ST, 1), (KV, 3), (ST, 2), (ST, 3))
+ORDER = ((KV, 0), (KV, 1), (KV, 2), (CR, 0), (ST, 0), (ST, 1), (ST, 2), (ST, 3), (KV, 3))
 LEFT = ((KV, 0), (KV, 1), (ST, 0), (ST, 1))
 
 
@@ -302,7 +302,8 @@
                 else:
                     old = peak[slot]
                     new = jnp.maximum(old, top)
-                peak[slot] = new
+                if first_time:
+                    peak[slot] = new
                 wide_new = jnp.concatenate([new] * (s.shape[1] // 128), axis=1)
                 prob = jnp.exp2((s - wide_new) * SCALE2).astype(BF16)
                 ones = jnp.ones((values.shape[0], 128), BF16)
@@ -310,7 +311,12 @@
                 if not first_time:
                     back = jnp.exp2((old - new) * SCALE2)
                     out = out + acc[slot] * jnp.concatenate([back, back], axis=1)
-                acc[slot] = out
+                    done = (out[:, 0:128] / out[:, 128:256]).astype(BF16)
+                    for e in range(2):
+                        lanes_out = pl.ds(pl.multiple_of((h + e) * 128, 128), 128)
+                        attn_out[rows, lanes_out] = done[e * BLK : (e + 1) * BLK]
+                else:
+                    acc[slot] = out
                 return 0
 
             lax.fori_loop(0, 4, one, 0, unroll=UNROLL)
@@ -345,8 +351,8 @@
             squares[i] = squares[i] + jnp.sum(gated * gated, axis=1, keepdims=True)
         return squares
 
-    near_at = {0: 0, 1: 1, 2: 2, 6: 3}
-    rest_at = {7: 0, 8: 1}
+    near_at = {0: 0, 1: 1, 2: 2, 8: 3}
+    rest_at = {6: 0, 7: 1}
     for i, item in enumerate(ORDER):
         got4(item)
         got1(item)
@@ -369,31 +375,19 @@
     for quarter in (0, 1):
         got2((ST, quarter))
         squares = finish_ssm(quarter, squares)
-    for g in (2, 3):
-        got2((KV, g))
-        attend(g, rest, False)
+    got2((KV, 2))
+    attend(2, rest, False)
     for quarter in (2, 3):
         got2((ST, quarter))
         squares = finish_ssm(quarter, squares)
     for i in range(2):
         sq_own[i * BLK : (i + 1) * BLK] = jnp.broadcast_to(squares[i], (BLK, 128))
-
     sq_copy = pltpu.make_async_remote_copy(
         sq_own, sq_other, qsem.at[0], qsem.at[1], device_id=other, device_id_type=MESH
     )
+    got2((KV, 3))
     sq_copy.start()
-
-    def divide(t, _):
-        for half in range(2):
-            rows = slice(half * BLK, (half + 1) * BLK)
-            slot = half * 16 + t
-            for e in range(2):
-                part = slice(e * BLK, (e + 1) * BLK)
-                lanes = pl.ds(pl.multiple_of((2 * t + e) * 128, 128), 128)
-                attn_out[rows, lanes] = (acc[slot, part, 0:128] / acc[slot, part, 128:256]).astype(BF16)
-        return 0
-
-    lax.fori_loop(0, 16, divide, 0)
+    attend(3, rest, False)
     sq_copy.wait()
     for i in range(2):
         rows = slice(i * BLK, (i + 1) * BLK)
@@ -418,8 +412,8 @@
     return pl.pallas_call(
         body,
         out_shape=(
-            jax.ShapeDtypeStruct((ROWS, LANES), BF16),
-            jax.ShapeDtypeStruct((ROWS, 4096), BF16),
+            pltpu.VMEM((ROWS, LANES), BF16),
+            pltpu.VMEM((ROWS, 4096), BF16),
         ),
         in_specs=[sm] + [vm] * 9 + [hbm] * 2,
         out_specs=(vm, vm),

time: 68.2 us -> 63.9 us (0.937)
  Pallas kernels: 63.7 us -> 60.8 us
  local copies, waits for them, and re-layouts: 3.78 us -> 2.29 us
    pallas_call x1, Pallas kernels: 63.7 us -> 60.8 us  [per_device(): pl.pallas_call(body, out_shape=(pltpu.VMEM((ROWS, LANES), BF16), pltpu.VM...]
    unnamed x4 -> x2, local copies, waits for them, and re-layouts: 3.78 us -> 2.29 us
where the time goes in v2:
time: 63.9 us; the launch traced here: 63.7 us
  Pallas kernels  60.8 us (95%)
  local copies, waits for them, and re-layouts  2.29 us (4%)
  between operations  0.64 us (1%)
    pallas_call x1, Pallas kernels, per_device(): pl.pallas_call(body, out_shape=(pltpu.VMEM((ROWS, LANES), BF16), pltpu.VM...  60.8 us
    unnamed x2, local copies, waits for them, and re-layouts  2.29 us

profile of v2, /device:TPU:1, one launch (start us, length us, event | category | flops | bytes accessed | tf_op | source)
XLA Modules:
  0.0 63.7 jit_solution(14298254017581465432)
XLA Ops:
  0.6 60.8 %layer.1 = (bf16[256,2048]{1,0:T(8,128)(2,1)S(1)}, bf16[256,4096]{1,0:T(8,128)(2,1)S(1)}) custom-call(s32[32]{0:T(128)} %doc_ref.1, bf16[256,2048]{1,0:T(8,128)(2,1)} %x_ref.1, bf16[256,256]{1,0:T(8,128)(2,1)} %b_ref.1, bf16[256,256]{1,0:T(8,128)(2,1)} %c_ref.1, f32[32,256]{1,0:T(8,128)} %bitcast.4, f32[32,256]{1,0:T(8,128)} %bitcast.5, f32[1,32]{1,0:T(1,128)} %bitcast.7, ...), custom_call_target="tpu_custom_call" | custom-call | tf_op jit(solution)/shard_map/layer/pallas_call | solution.py:412
  61.4 1.0 %copy.16 = bf16[256,2048]{1,0:T(8,128)(2,1)} copy(bf16[256,2048]{1,0:T(8,128)(2,1)S(1)} %get-tuple-element.2) | data formatting | bytes 2097152
  62.4 1.3 %copy.17 = bf16[256,4096]{1,0:T(8,128)(2,1)} copy(bf16[256,4096]{1,0:T(8,128)(2,1)S(1)} %get-tuple-element.3) | data formatting | bytes 4194304

commit v3 on v2

--- a/solution.py
+++ b/solution.py
@@ -43,9 +43,9 @@
 
 
 def body(
-    doc_ref, x_ref, b_ref, c_ref, step_ref, decay_ref, skip_ref, gain_ref, k_ref, v_ref, z_hbm, q_hbm,
+    doc_ref, x_hbm, b_ref, c_ref, step_ref, decay_ref, skip_ref, gain_ref, k_ref, v_ref, z_hbm, q_hbm,
     ssm_out, attn_out,
-    z_ref, q_ref, kbuf, vbuf, tbuf, cbuf, town, cown, qaug, kaug, acc, peak,
+    x_ref, z_ref, q_ref, kbuf, vbuf, tbuf, cbuf, town, cown, qaug, kaug, acc, peak,
     dpad, spad, skip_pad, cum3, cum_t, step_t, end_t, scm, bt, intra, rgain, spread, bs0, enter0, enter1,
     sq_own, sq_other,
     lsem, kvs, kvr, sts, str_, qsem,
@@ -63,6 +63,8 @@
     other = {"head": 1 - head}
     z_copy = pltpu.make_async_copy(z_hbm, z_ref, lsem.at[0])
     q_copy = pltpu.make_async_copy(q_hbm, q_ref, lsem.at[1])
+    x_copy = pltpu.make_async_copy(x_hbm, x_ref, lsem.at[2])
+    x_copy.start()
     q_copy.start()
     z_copy.start()
     barrier = pltpu.get_barrier_semaphore()
@@ -85,18 +87,19 @@
                 for own, buf, j in pairs
             ]
         if kind == ST:
-            lanes = pl.ds(i * 512, 512)
+            halves = [pl.ds(i * 512 + j * 256, 256) for j in range(2)]
             return [
                 pltpu.make_async_remote_copy(
                     town.at[:, lanes] if src == 0 else tbuf.at[src - 1, :, lanes],
                     tbuf.at[dist - 1, :, lanes],
-                    sts.at[s, i], str_.at[r, i], device_id=to, device_id_type=MESH,
+                    sts.at[s, i, j], str_.at[r, i, j], device_id=to, device_id_type=MESH,
                 )
+                for j, lanes in enumerate(halves)
             ]
         return [
             pltpu.make_async_remote_copy(
                 cown if src == 0 else cbuf.at[src - 1], cbuf.at[dist - 1],
-                sts.at[s, 4], str_.at[r, 4], device_id=to, device_id_type=MESH,
+                sts.at[s, 4, 0], str_.at[r, 4, 0], device_id=to, device_id_type=MESH,
             )
         ]
 
@@ -122,26 +125,32 @@
             for item in items:
                 start(send(item, 0, 3, left))
 
+    def parts_of(item):
+        return range(1 if item[0] == CR else 2)
+
     def got4(item):
-        arrive(item, 4)
-
-        @pl.when(x > 0)
-        def _():
-            start(send(item, 4, 3, left))
-
-        @pl.when(x == 3)
-        def _():
-            start(send(item, 4, 1, right))
+        for j in parts_of(item):
+            send(item, 0, 4, at(4))[j].wait_recv()
+
+            @pl.when(x > 0)
+            def _():
+                send(item, 4, 3, left)[j].start()
+
+            @pl.when(x == 3)
+            def _():
+                send(item, 4, 1, right)[j].start()
 
     def got1(item):
-        arrive(item, 1)
-        if item not in LEFT:
-            start(send(item, 1, 2, at(1)))
+        for j in parts_of(item):
+            send(item, 0, 1, at(4))[j].wait_recv()
+            if item not in LEFT:
+                send(item, 1, 2, at(1))[j].start()
 
     def got3(item):
-        arrive(item, 3)
-        if item in LEFT:
-            start(send(item, 3, 2, at(-1)))
+        for j in parts_of(item):
+            send(item, 0, 3, at(4))[j].wait_recv()
+            if item in LEFT:
+                send(item, 3, 2, at(-1))[j].start()
 
     def got2(item):
         arrive(item, 2)
@@ -264,7 +273,8 @@
         town[:, lanes] = (c1 * outs[0] + outs[1]).astype(BF16)
         return 0
 
-    lax.fori_loop(0, PAIRS, pair, 0)
+    x_copy.wait()
+    lax.fori_loop(0, PAIRS, pair, 0, unroll=2)
     send_own(ORDER[3:6])
     q_copy.wait()
 
@@ -415,9 +425,10 @@
             pltpu.VMEM((ROWS, LANES), BF16),
             pltpu.VMEM((ROWS, 4096), BF16),
         ),
-        in_specs=[sm] + [vm] * 9 + [hbm] * 2,
+        in_specs=[sm, hbm] + [vm] * 8 + [hbm] * 2,
         out_specs=(vm, vm),
         scratch_shapes=[
+            pltpu.VMEM((ROWS, LANES), BF16),
             pltpu.VMEM((ROWS, LANES), BF16),
             pltpu.VMEM((ROWS, 4096), BF16),
             pltpu.VMEM((4, ROWS, 512), BF16),
@@ -447,11 +458,11 @@
             pltpu.VMEM((8, LANES), F32),
             pltpu.VMEM((ROWS, 128), F32),
             pltpu.VMEM((ROWS, 128), F32),
-            dma((2,)),
+            dma((3,)),
             dma((4, 4, 2)),
             dma((4, 4, 2)),
-            dma((4, 5)),
-            dma((4, 5)),
+            dma((4, 5, 2)),
+            dma((4, 5, 2)),
             dma((2,)),
         ],
         compiler_params=pltpu.CompilerParams(collective_id=0, has_side_effects=True),

time: 63.9 us -> 62.8 us (0.983)
  Pallas kernels: 60.8 us -> 59.7 us
    pallas_call x1, Pallas kernels: 60.8 us -> 59.7 us  [per_device(): pl.pallas_call(body, out_shape=(pltpu.VMEM((ROWS, LANES), BF16), pltpu.VM...]
where the time goes in v3:
time: 62.8 us; the launch traced here: 62.6 us
  Pallas kernels  59.7 us (95%)
  local copies, waits for them, and re-layouts  2.29 us (4%)
  between operations  0.64 us (1%)
    pallas_call x1, Pallas kernels, per_device(): pl.pallas_call(body, out_shape=(pltpu.VMEM((ROWS, LANES), BF16), pltpu.VM...  59.7 us
    unnamed x2, local copies, waits for them, and re-layouts  2.29 us

profile of v3, /device:TPU:1, one launch (start us, length us, event | category | flops | bytes accessed | tf_op | source)
XLA Modules:
  0.0 62.6 jit_solution(15544536169237840169)
XLA Ops:
  0.6 59.7 %layer.1 = (bf16[256,2048]{1,0:T(8,128)(2,1)S(1)}, bf16[256,4096]{1,0:T(8,128)(2,1)S(1)}) custom-call(s32[32]{0:T(128)} %doc_ref.1, bf16[256,2048]{1,0:T(8,128)(2,1)} %x_hbm.1, bf16[256,256]{1,0:T(8,128)(2,1)} %b_ref.1, bf16[256,256]{1,0:T(8,128)(2,1)} %c_ref.1, f32[32,256]{1,0:T(8,128)} %bitcast.4, f32[32,256]{1,0:T(8,128)} %bitcast.5, f32[1,32]{1,0:T(1,128)} %bitcast.7, ...), custom_call_target="tpu_custom_call" | custom-call | tf_op jit(solution)/shard_map/layer/pallas_call | solution.py:422
  60.4 1.0 %copy.16 = bf16[256,2048]{1,0:T(8,128)(2,1)} copy(bf16[256,2048]{1,0:T(8,128)(2,1)S(1)} %get-tuple-element.2) | data formatting | bytes 2097152
  61.3 1.3 %copy.17 = bf16[256,4096]{1,0:T(8,128)(2,1)} copy(bf16[256,4096]{1,0:T(8,128)(2,1)S(1)} %get-tuple-element.3) | data formatting | bytes 4194304
